TPU v7x, 32 devices: a whole 2x2x4 slice. The times are simulated.
32 devices in a mesh: blk: 8 (over y, x, core), fsdp: 4 (over z).
Axes of the slice: x: 2, y: 2, z: 4, core: 2. Of those that a mesh axis runs over, the one named last changes fastest.
Arguments:
- x_forward: bfloat16 [8192, 4096], P(('blk', 'fsdp'))
- seg_forward: int32 [32, 256], P(('blk', 'fsdp')), may hold values from 0 to 3, never falling along the last dimension, each value on 1 to 128 neighbouring positions
- x_saved: bfloat16 [8192, 4096], P(('blk', 'fsdp'))
- x_earlier: bfloat16 [8192, 4096], P(('blk', 'fsdp'))
- cotangent: bfloat16 [8192, 4096], P(('blk', 'fsdp')), may hold values from -0.119628906 to 0.119628906
- seg_backward: int32 [32, 256], P(('blk', 'fsdp')), may hold values from 0 to 3, never falling along the last dimension, each value on 1 to 128 neighbouring positions
- gain: bfloat16 [8, 4096], P('blk', 'fsdp'), may hold values from 0.25 to 1.75
- qkv: bfloat16 [8, 4096, 768], P('blk', 'fsdp')
- proj: bfloat16 [8, 512, 4096], P('blk', None, 'fsdp'), may hold values from -0.25 to 0.25
- sum_gain: float32 [8, 4096], P('blk', 'fsdp'), may hold values from -6 to 6
- sum_qkv: float32 [8, 4096, 768], P('blk', 'fsdp'), may hold values from -6 to 6
- sum_proj: float32 [8, 512, 4096], P('blk', None, 'fsdp'), may hold values from -6 to 6
Outputs:
- hidden_out: bfloat16 [8192, 4096], P(('blk', 'fsdp'))
- new_sum_gain: float32 [8, 4096], P('blk', 'fsdp')
- new_sum_qkv: float32 [8, 4096, 768], P('blk', 'fsdp')
- new_sum_proj: float32 [8, 512, 4096], P('blk', None, 'fsdp')
Inputs may be any that keep to these rules, and one draw needn't show every extreme that they name: `seg_forward`: each row of ids never falls along the micro-batch. `seg_backward`: each row of ids never falls along the micro-batch.
All inputs are finite; a program needn't handle non-finite values.
Results may differ from a plain program's by a relative error of at most 0.018.
The roundings to bfloat16 on the way count: a program that leaves them out, or rounds other values in their place, can miss the bound.
Values may be sent and summed in bfloat16 or wider, within the bound.
No kernel may reach another device: no remote copies, remote signals or barrier semaphores. Data moves between devices by JAX's collectives and lax.ppermute only.
A program may use at most 192 MiB of HBM per device.

v0:
```python
import jax
import jax.numpy as jnp
from jax import lax
from jax.sharding import PartitionSpec as P

HEADS = 4
HEAD_DIM = 128


def shifted(value, axis, steps):
    count = lax.axis_size(axis)
    pairs = [(source, (source + steps) % count) for source in range(count)]
    return lax.ppermute(value, axis, pairs)


def attention_mask(segments):
    count = segments.shape[0]
    row_ids = lax.broadcasted_iota(jnp.int32, (count, count), 0)
    col_ids = lax.broadcasted_iota(jnp.int32, (count, count), 1)
    return (col_ids <= row_ids) & (segments[:, None] == segments[None, :])


def layer_parts(tokens, segments, norm_gain, qkv_weight):
    count = tokens.shape[0]
    att_width = HEADS * HEAD_DIM
    wide_rows = tokens.astype(jnp.float32)
    inv_rms = lax.rsqrt(jnp.mean(wide_rows * wide_rows, axis=1, keepdims=True) + 1e-05)
    normed = (wide_rows * inv_rms * norm_gain.astype(jnp.float32)[None, :]).astype(jnp.bfloat16)
    projected = jnp.dot(normed, qkv_weight, preferred_element_type=jnp.float32).astype(jnp.bfloat16)
    queries = projected[:, :att_width].reshape(count, HEADS, HEAD_DIM)
    key_rows = projected[:, att_width : att_width + HEAD_DIM]
    values = projected[:, att_width + HEAD_DIM :]
    score_scale = HEAD_DIM ** (-0.5)
    scores = (
        jnp.einsum("thd,sd->hts", queries, key_rows, preferred_element_type=jnp.float32)
        * score_scale
    )
    allowed = attention_mask(segments)[None]
    scores = jnp.where(allowed, scores, -1e30)
    row_max = jnp.max(scores, axis=2, keepdims=True)
    expo = jnp.where(allowed, jnp.exp(scores - row_max), 0.0)
    attn_probs = expo / jnp.sum(expo, axis=2, keepdims=True)
    attn_low = attn_probs.astype(jnp.bfloat16)
    attended = jnp.einsum("hts,sd->thd", attn_low, values, preferred_element_type=jnp.float32)
    attended = attended.reshape(count, att_width).astype(jnp.bfloat16)
    return (wide_rows, inv_rms, normed, queries, key_rows, values, attn_probs, attn_low, attended)


def layer_forward(tokens, segments, layer_weights):
    norm_gain, qkv_weight, proj_weight = layer_weights
    pieces_all = layer_parts(tokens, segments, norm_gain, qkv_weight)
    branch_out = jnp.dot(pieces_all[8], proj_weight, preferred_element_type=jnp.float32)
    return (pieces_all[0] + branch_out).astype(jnp.bfloat16)


def layer_backward(tokens, segments, layer_weights, upstream, with_input):
    norm_gain, qkv_weight, proj_weight = layer_weights
    wide_rows, inv_rms, normed, queries, key_rows, values, attn_probs, attn_low, attended = (
        layer_parts(tokens, segments, norm_gain, qkv_weight)
    )
    count = tokens.shape[0]
    d_att = lax.dot_general(
        upstream, proj_weight, (((1,), (1,)), ((), ())), preferred_element_type=jnp.float32
    ).astype(jnp.bfloat16)
    grad_proj = lax.dot_general(
        attended, upstream, (((0,), (0,)), ((), ())), preferred_element_type=jnp.float32
    )
    d_heads = d_att.reshape(count, HEADS, HEAD_DIM)
    d_probs = jnp.einsum("thd,sd->hts", d_heads, values, preferred_element_type=jnp.float32)
    grad_values = jnp.einsum("hts,thd->sd", attn_low, d_heads, preferred_element_type=jnp.float32)
    row_inner = jnp.sum(d_probs * attn_probs, axis=2, keepdims=True)
    d_scores = (attn_probs * (d_probs - row_inner) * HEAD_DIM ** (-0.5)).astype(jnp.bfloat16)
    grad_queries = jnp.einsum(
        "hts,sd->thd", d_scores, key_rows, preferred_element_type=jnp.float32
    ).reshape(count, HEADS * HEAD_DIM)
    grad_keys = jnp.einsum("hts,thd->sd", d_scores, queries, preferred_element_type=jnp.float32)
    d_projected = jnp.concatenate([grad_queries, grad_keys, grad_values], axis=1).astype(
        jnp.bfloat16
    )
    grad_qkv = lax.dot_general(
        normed, d_projected, (((0,), (0,)), ((), ())), preferred_element_type=jnp.float32
    )
    d_normed = lax.dot_general(
        d_projected, qkv_weight, (((1,), (1,)), ((), ())), preferred_element_type=jnp.float32
    )
    grad_gain = jnp.sum(d_normed * wide_rows * inv_rms, axis=0)
    grad_terms = (grad_gain, grad_qkv, grad_proj)
    if not with_input:
        return (grad_terms, upstream)
    scaled = d_normed * norm_gain.astype(jnp.float32)[None, :]
    d_wide = inv_rms * scaled - wide_rows * inv_rms**3 * jnp.mean(
        scaled * wide_rows, axis=1, keepdims=True
    )
    d_tokens = (upstream.astype(jnp.float32) + d_wide).astype(jnp.bfloat16)
    return (grad_terms, d_tokens)


def gather_layer(gain_piece, qkv_piece, proj_piece):
    gathered = (
        lax.all_gather(gain_piece, "fsdp", axis=1, tiled=True),
        lax.all_gather(qkv_piece, "fsdp", axis=1, tiled=True),
        lax.all_gather(proj_piece, "fsdp", axis=2, tiled=True),
    )
    return (gathered[0][0], gathered[1][0], gathered[2][0])


def reduce_terms(grad_terms):
    return (
        lax.psum_scatter(
            grad_terms[0][None].astype(jnp.bfloat16), "fsdp", scatter_dimension=1, tiled=True
        ).astype(jnp.float32),
        lax.psum_scatter(
            grad_terms[1][None].astype(jnp.bfloat16), "fsdp", scatter_dimension=1, tiled=True
        ).astype(jnp.float32),
        lax.psum_scatter(
            grad_terms[2][None].astype(jnp.bfloat16), "fsdp", scatter_dimension=2, tiled=True
        ).astype(jnp.float32),
    )


def body(
    x_forward,
    seg_forward,
    x_saved,
    x_earlier,
    cotangent,
    seg_backward,
    gain,
    qkv,
    proj,
    sum_gain,
    sum_qkv,
    sum_proj,
):
    ids_fwd = seg_forward[0]
    ids_bwd = seg_backward[0]
    layer_now = gather_layer(gain, qkv, proj)
    hidden = layer_forward(x_forward, ids_fwd, layer_now)
    terms_one, d_hidden = layer_backward(x_saved, ids_bwd, layer_now, cotangent, True)
    sums_one = reduce_terms(terms_one)
    carried = (
        shifted((sum_gain + sums_one[0]).astype(jnp.bfloat16), "blk", 1).astype(jnp.float32),
        shifted((sum_qkv + sums_one[1]).astype(jnp.bfloat16), "blk", 1).astype(jnp.float32),
        shifted((sum_proj + sums_one[2]).astype(jnp.bfloat16), "blk", 1).astype(jnp.float32),
    )
    layer_next = shifted((layer_now[0], layer_now[1], layer_now[2]), "blk", 1)
    result = layer_forward(hidden, ids_fwd, layer_next)
    terms_two, unused = layer_backward(x_earlier, ids_bwd, layer_next, d_hidden, False)
    sums_two = reduce_terms(terms_two)
    return (result, carried[0] + sums_two[0], carried[1] + sums_two[1], carried[2] + sums_two[2])


def solution(mesh):
    in_specs = (
        P(("blk", "fsdp"), None),
        P(("blk", "fsdp"), None),
        P(("blk", "fsdp"), None),
        P(("blk", "fsdp"), None),
        P(("blk", "fsdp"), None),
        P(("blk", "fsdp"), None),
        P("blk", "fsdp"),
        P("blk", "fsdp", None),
        P("blk", None, "fsdp"),
        P("blk", "fsdp"),
        P("blk", "fsdp", None),
        P("blk", None, "fsdp"),
    )
    out_specs = (
        P(("blk", "fsdp"), None),
        P("blk", "fsdp"),
        P("blk", "fsdp", None),
        P("blk", None, "fsdp"),
    )
    return jax.shard_map(body, mesh=mesh, in_specs=in_specs, out_specs=out_specs, check_vma=False)
```

profile of v0, /device:TPU:0, one launch (start us, length us, event | category | flops | bytes accessed | tf_op | source)
XLA Modules:
  0.0 684.2 jit_solution(11718930285268044913)
XLA Ops:
  7.2 0.7 all-gather.5.cloned.1.call-update
  8.0 0.7 all-gather.3.cloned.1.call-update
  8.7 15.1 %all_gather.9 = bf16[1,4096]{1,0:T(2,128)(2,1)S(1)} all-gather(bf16[1,1024]{1,0:T(2,128)(2,1)} %param.18), channel_id=1, replica_groups=mesh['blk'=8,'fsdp'=4] {'fsdp'}, dimensions={1}, use_global_device_ids=true | all-gather | bytes 10240 | tf_op jit(solution)/shard_map/all_gather | solution.py:100
  23.8 2.1 fusion.22
  26.0 67.0 %all-gather.5.cloned.1.call-done = bf16[1,512,4096]{2,1,0:T(8,128)(2,1)} async-done(((bf16[1,512,1024]{2,1,0:T(8,128)(2,1)}), bf16[1,512,4096]{2,1,0:T(8,128)(2,1)}) %all-gather.5.cloned.1.call-update) | async-done | bytes 4194320 | tf_op jit(solution)/shard_map/all_gather | solution.py:102
  93.1 3.5 convolution_convert_fusion.11
  96.5 0.1 copy.95
  96.7 111.8 %all-gather.3.cloned.1.call-done = bf16[1,4096,768]{2,1,0:T(8,128)(2,1)} async-done(((bf16[1,1024,768]{2,1,0:T(8,128)(2,1)}), bf16[1,4096,768]{2,1,0:T(8,128)(2,1)}) %all-gather.3.cloned.1.call-update) | async-done | bytes 6291472 | tf_op jit(solution)/shard_map/all_gather | solution.py:101
  208.5 5.3 convolution_convert_fusion.5
  213.8 0.9 copy.94
  214.6 1.1 convolution_bitcast_fusion.1
  215.8 2.5 fusion.169
  218.3 2.4 fusion.76
  220.7 2.2 fusion.75
  223.0 2.9 convolution_convert_fusion.10
  225.9 8.1 %fusion.26 = (bf16[4096]{0:T(1024)(128)(2,1)S(1)}, f32[256]{0:T(256)S(1)}, f32[256,4096]{1,0:T(8,128)}) fusion(bf16[256,4096]{1,0:T(8,128)(2,1)} %param.14, f32[256]{0:T(256)S(1)} %get-tuple-element.7, f32[4096]{0:T(1024)S(1)} %mul.172, bf16[1,4096,768]{2,1,0:T(8,128)(2,1)} %all-gather.3.cloned.1.call-done, bf16[256,128]{0,1:T(8,128)(2,1)S(1)} %copy-done.15, ...), kind=kOutput, calls=%fused_computation.44 | convolution fusion | flops 1619128064 | bytes 13002752 | tf_op jit(solution)/shard_map/dot_general | solution.py:83
  234.0 1.6 reshape_bitcast_fusion.1
  235.6 6.2 fusion.6
  242.0 0.8 copy-done.10
  242.8 1.6 convolution_convert_fusion.7
  244.4 3.2 fusion.8
  247.7 0.8 collective-permute-start.2
  248.5 1.1 collective-permute-start
  249.6 2.1 fusion.19
  251.7 106.7 %collective-permute-done = bf16[4096]{0:T(1024)(128)(2,1)S(1)} collective-permute-done((bf16[4096]{0:T(1024)(128)(2,1)S(1)}, bf16[4096]{0:T(1024)(128)(2,1)S(1)}, u32[]{:S(2)}, u32[]{:S(2)}) %collective-permute-start) | collective-permute-done | bytes 8224 | tf_op jit(solution)/shard_map/ppermute | solution.py:13
  358.5 4.4 fusion.30
  362.9 1.3 copy-done.3
  364.2 2.0 copy-done.5
  366.2 1.3 convolution_convert_fusion.9
  367.7 4.6 convolution_convert_fusion.4
  372.5 0.3 convolution_bitcast_fusion
  372.8 1.5 fusion.170
  374.3 2.2 fusion.77
  376.5 2.2 convolution_convert_fusion.8
  378.8 0.8 fusion.78
  379.6 0.8 convolution_convert_fusion.6
  380.4 6.6 fusion.40
  387.0 1.6 reshape_bitcast_fusion
  388.7 3.2 fusion.9
  391.9 0.2 reduce-scatter.13.cloned.1.call-start
  392.1 1.3 copy-done.8
  393.5 4.6 fusion.7
  398.1 1.6 copy-done
  399.7 0.5 fusion.13
  400.3 4.7 fusion.69
  405.0 0.6 fusion.163
  405.6 0.8 convolution_convert_fusion.13
  406.4 5.1 fusion.16
  411.5 1.1 copy.91
  412.7 6.2 fusion.72
  418.9 2.9 add_convert_fusion
  421.8 0.8 collective-permute-start.4
  422.6 29.5 %reduce-scatter.15.cloned.1.call-done = bf16[1,512,1024]{2,1,0:T(8,128)(2,1)} async-done(((bf16[1,512,4096]{2,1,0:T(8,128)(2,1)}), bf16[1,512,1024]{2,1,0:T(8,128)(2,1)}) %reduce-scatter.15.cloned.1.call-update) | async-done | bytes 1048592 | tf_op jit(solution)/shard_map/reduce_scatter | solution.py:115
  452.1 3.2 add_convert_fusion.1
  455.3 1.7 fusion.166
  457.0 1.8 convolution_convert_fusion.12
  458.8 4.9 fusion.12
  463.7 18.3 %reduce-scatter.21.cloned.1.call-done = bf16[1024,1]{1,0:T(8,128)(2,1)} async-done(((bf16[4096,1]{1,0:T(8,128)(2,1)}), bf16[1024,1]{1,0:T(8,128)(2,1)}) %reduce-scatter.21.cloned.1.call-update) | async-done | bytes 2064
  482.1 1.1 copy.93
  483.2 0.6 convert_add_fusion.4
  483.8 75.9 %reduce-scatter.17.cloned.1.call-done = bf16[1,512,1024]{2,1,0:T(8,128)(2,1)} async-done(((bf16[1,512,4096]{2,1,0:T(8,128)(2,1)}), bf16[1,512,1024]{2,1,0:T(8,128)(2,1)}) %reduce-scatter.17.cloned.1.call-update) | async-done | bytes 1048592 | tf_op jit(solution)/shard_map/reduce_scatter | solution.py:115
  559.7 2.9 convert_add_fusion.3
  562.6 110.7 %reduce-scatter.13.cloned.1.call-done = bf16[1,1024,768]{2,1,0:T(8,128)(2,1)} async-done(((bf16[1,4096,768]{2,1,0:T(8,128)(2,1)}), bf16[1,1024,768]{2,1,0:T(8,128)(2,1)}) %reduce-scatter.13.cloned.1.call-update) | async-done | bytes 1572880 | tf_op jit(solution)/shard_map/reduce_scatter | solution.py:112
  673.3 3.9 convert_add_fusion.2
  (65 shorter events, 1.2 us)
Async XLA Ops:
  7.2 18.8 %copy-start.12 = (s32[1,256]{1,0:T(1,128)S(1)}, s32[1,256]{1,0:T(1,128)}, u32[]{:S(2)}) copy-start(s32[1,256]{1,0:T(1,128)} %param.17) | copy-start | bytes 3076
  7.2 85.9 %copy-start.1 = (bf16[256,4096]{1,0:T(8,128)(2,1)S(1)}, bf16[256,4096]{1,0:T(8,128)(2,1)}, u32[]{:S(2)}) copy-start(bf16[256,4096]{1,0:T(8,128)(2,1)} %param.16) | copy-start | bytes 6291460
  7.2 85.9 %all-gather.5.cloned.1.call-start = ((), (), s32[]{:S(2)}) async-start(), calls=%async_computation.7 | async-start | bytes 5242880 | tf_op jit(solution)/shard_map/all_gather | solution.py:102
  7.9 200.6 %all-gather.3.cloned.1.call-start = ((), (), s32[]{:S(2)}) async-start(), calls=%async_computation.6 | async-start | bytes 7864320 | tf_op jit(solution)/shard_map/all_gather | solution.py:101
  8.7 402.8 %reduce-scatter.19.cloned.1.call-start = ((), (), s32[]{:S(2)}) async-start(), calls=%async_computation.12 | async-start | bytes 1310720
  213.7 0.9 copy-start.9
  220.7 5.2 copy-start.15
  225.9 9.7 %copy-start.14 = (bf16[128,4,256]{2,0,1:T(8,128)(2,1)S(1)}, bf16[128,4,256]{2,0,1:T(8,128)(2,1)}, u32[]{:S(2)}) copy-start(bf16[128,4,256]{2,0,1:T(8,128)(2,1)} %convolution_convert_fusion.10) | copy-start | bytes 786436
  235.6 183.3 %reduce-scatter.11.cloned.1.call-start = ((), (), s32[]{:S(2)}) async-start(), calls=%async_computation.8 | async-start | bytes 7864320 | tf_op jit(solution)/shard_map/reduce_scatter | solution.py:112
  241.8 0.9 copy-start.10
  241.8 210.3 %reduce-scatter.15.cloned.1.call-start = ((), (), s32[]{:S(2)}) async-start(), calls=%async_computation.10 | async-start | bytes 5242880 | tf_op jit(solution)/shard_map/reduce_scatter | solution.py:115
  241.9 125.8 %collective-permute-start.1 = (bf16[4096,768]{1,0:T(8,128)(2,1)}, bf16[4096,768]{1,0:T(8,128)(2,1)}, u32[]{:S(2)}, u32[]{:S(2)}) collective-permute-start(bf16[4096,768]{1,0:T(8,128)(2,1)} %bitcast.308), channel_id=1, source_target_pairs={{0,4},{4,8},{8,12},{12,16},{16,20},{20,24},{24,28},{28,0},{1,5},{5... | collective-permute-start | bytes 18874376 | tf_op jit(solution)/shard_map/ppermute | solution.py:13
  247.6 234.4 %reduce-scatter.21.cloned.1.call-start = ((), (), s32[]{:S(2)}) async-start(), calls=%async_computation.13 | async-start | bytes 1310720
  247.7 115.2 %collective-permute-start.2 = (bf16[512,4096]{1,0:T(8,128)(2,1)}, bf16[512,4096]{1,0:T(8,128)(2,1)S(1)}, u32[]{:S(2)}, u32[]{:S(2)}) collective-permute-start(bf16[512,4096]{1,0:T(8,128)(2,1)} %bitcast.287), channel_id=1, source_target_pairs={{0,4},{4,8},{8,12},{12,16},{16,20},{20,24},{24,28},{28,0},{1,5},{5... | collective-permute-start | bytes 12582920 | tf_op jit(solution)/shard_map/ppermute | solution.py:13
  248.5 110.0 %collective-permute-start = (bf16[4096]{0:T(1024)(128)(2,1)S(1)}, bf16[4096]{0:T(1024)(128)(2,1)S(1)}, u32[]{:S(2)}, u32[]{:S(2)}) collective-permute-start(bf16[4096]{0:T(1024)(128)(2,1)S(1)} %reduce), channel_id=1, source_target_pairs={{0,4},{4,8},{8,12},{12,16},{16,20},{20,24},{24,28},{28,0},{1,5},{5... | collective-permute-start | bytes 24584 | tf_op jit(solution)/shard_map/ppermute | solution.py:13
  362.9 1.3 copy-start.3
  362.9 4.8 copy-start.7
  364.2 2.0 copy-start.5
  380.4 8.3 %copy-start.4 = (bf16[256,4096]{1,0:T(8,128)(2,1)S(1)}, bf16[256,4096]{1,0:T(8,128)(2,1)}, u32[]{:S(2)}) copy-start(bf16[256,4096]{1,0:T(8,128)(2,1)} %copy-done.3) | copy-start | bytes 6291460
  388.6 171.1 %reduce-scatter.17.cloned.1.call-start = ((), (), s32[]{:S(2)}) async-start(), calls=%async_computation.11 | async-start | bytes 5242880 | tf_op jit(solution)/shard_map/reduce_scatter | solution.py:115
  391.9 1.6 copy-start.8
  391.9 281.4 %reduce-scatter.13.cloned.1.call-start = ((), (), s32[]{:S(2)}) async-start(), calls=%async_computation.9 | async-start | bytes 7864320 | tf_op jit(solution)/shard_map/reduce_scatter | solution.py:112
  398.1 1.6 copy-start
  398.1 2.1 copy-start.13
  406.4 6.2 copy-start.11
  412.6 70.5 %collective-permute-start.3 = (bf16[1,1024]{1,0:T(2,128)(2,1)S(1)}, bf16[1,1024]{1,0:T(2,128)(2,1)S(1)}, u32[]{:S(2)}, u32[]{:S(2)}) collective-permute-start(bf16[1,1024]{1,0:T(2,128)(2,1)S(1)} %add_convert_fusion.2), channel_id=1, source_target_pairs={{0,4},{4,8},{8,12},{12,16},{16,20},{20,24},{24,28},{28,0},{1,5},{5... | collective-permute-start | bytes 6152 | tf_op jit(solution)/shard_map/ppermute | solution.py:13
  412.7 6.2 copy-start.6
  421.8 140.9 %collective-permute-start.4 = (bf16[1,1024,768]{2,1,0:T(8,128)(2,1)}, bf16[1,1024,768]{2,1,0:T(8,128)(2,1)}, u32[]{:S(2)}, u32[]{:S(2)}) collective-permute-start(bf16[1,1024,768]{2,1,0:T(8,128)(2,1)} %add_convert_fusion), channel_id=1, source_target_pairs={{0,4},{4,8},{8,12},{12,16},{16,20},{20,24},{24,28},{28,0},{1,5},{5... | collective-permute-start | bytes 4718600 | tf_op jit(solution)/shard_map/ppermute | solution.py:13
  455.3 3.5 copy-start.2
  455.3 28.5 %collective-permute-start.5 = (bf16[1,512,1024]{2,1,0:T(8,128)(2,1)}, bf16[1,512,1024]{2,1,0:T(8,128)(2,1)S(1)}, u32[]{:S(2)}, u32[]{:S(2)}) collective-permute-start(bf16[1,512,1024]{2,1,0:T(8,128)(2,1)} %add_convert_fusion.1), channel_id=1, source_target_pairs={{0,4},{4,8},{8,12},{12,16},{16,20},{20,24},{24,28},{28,0},{1,5},{5... | collective-permute-start | bytes 3145736 | tf_op jit(solution)/shard_map/ppermute | solution.py:13
Sparse Core Ops, SparseCore 0:
  9.6 83.4 all-gather.4
  94.6 113.8 all-gather.2
  235.7 25.4 reduce-scatter.18
  263.3 109.2 reduce-scatter.10
  374.8 77.2 reduce-scatter.14
  454.3 27.7 reduce-scatter.20
  484.4 75.2 reduce-scatter.16
  562.0 111.2 reduce-scatter.12
where the time goes:
time: 694 us; the launch traced here: 684 us
  waiting for transfers between devices  522 us (75%)
  matrix products  93 us (13%)
  other arithmetic  22.9 us (3%)
  blocking collectives  15.1 us (2%)
  between operations  14.7 us (2%)
  local copies, waits for them, and re-layouts  13.8 us (2%)
    all_gather x1, waiting for transfers between devices, gather_layer(): lax.all_gather(qkv_piece, 'fsdp', axis=1, tiled=True)  112 us
    reduce_scatter x2, waiting for transfers between devices, reduce_terms(): lax.psum_scatter(grad_terms[1][None].astype(jnp.bfloat16), 'fsdp', scatte...  111 us
    ppermute x6, waiting for transfers between devices, shifted(): return lax.ppermute(value, axis, pairs)  107 us
    reduce_scatter x2, waiting for transfers between devices, reduce_terms(): lax.psum_scatter(grad_terms[2][None].astype(jnp.bfloat16), 'fsdp', scatte...  105 us
    all_gather x1, waiting for transfers between devices, gather_layer(): lax.all_gather(proj_piece, 'fsdp', axis=2, tiled=True)  67 us
    dot_general x4, matrix products, layer_parts(): jnp.dot(normed, qkv_weight, preferred_element_type=jnp.float32)  20.8 us
    unnamed x10, waiting for transfers between devices  19.8 us
    all_gather x1, blocking collectives, gather_layer(): lax.all_gather(gain_piece, 'fsdp', axis=1, tiled=True)  15.1 us
  transfers between devices with their start and end apart: 14, of which 7 were waited for; matrix products, arithmetic and copies ran while one was open for 13% of the time, Pallas kernels for 0%

commit v1 on v0

v1 whole, which is shorter than its diff:
```python
import jax
import jax.numpy as jnp
from jax import lax
from jax.experimental import pallas as pl
from jax.experimental.pallas import tpu as pltpu
from jax.sharding import PartitionSpec as P

HEADS = 4
HEAD_DIM = 128
F32 = jnp.float32
BF16 = jnp.bfloat16


def shifted(value, axis, steps):
    count = lax.axis_size(axis)
    pairs = [(source, (source + steps) % count) for source in range(count)]
    return lax.ppermute(value, axis, pairs)


def contract(a, b, dim_a, dim_b):
    return lax.dot_general(a, b, (((dim_a,), (dim_b,)), ((), ())), preferred_element_type=F32)


def attend_kernel(proj_ref, col_ref, row_ref, att_ref, prob_ref):
    count = proj_ref.shape[0]
    width = HEADS * HEAD_DIM
    rows = lax.broadcasted_iota(jnp.int32, (count, count), 0)
    cols = lax.broadcasted_iota(jnp.int32, (count, count), 1)
    allowed = (cols <= rows) & (col_ref[...] == row_ref[0])
    keys = proj_ref[:, width : width + HEAD_DIM]
    values = proj_ref[:, width + HEAD_DIM :]
    for head in range(HEADS):
        part = slice(head * HEAD_DIM, (head + 1) * HEAD_DIM)
        scores = contract(proj_ref[:, part], keys, 1, 1) * HEAD_DIM ** (-0.5)
        scores = jnp.where(allowed, scores, -1e30)
        top = jnp.max(scores, axis=1, keepdims=True)
        expo = jnp.where(allowed, jnp.exp(scores - top), 0.0)
        probs = expo / jnp.sum(expo, axis=1, keepdims=True)
        prob_ref[head] = probs
        att_ref[:, part] = contract(probs.astype(BF16), values, 1, 0).astype(BF16)


def attend(projected, ids):
    micro, count = ids.shape
    width = projected.shape[1]
    att_width = HEADS * HEAD_DIM
    return pl.pallas_call(
        attend_kernel,
        grid=(micro,),
        in_specs=[
            pl.BlockSpec((count, width), lambda m: (m, 0)),
            pl.BlockSpec((count, 1), lambda m: (m, 0)),
            pl.BlockSpec((1, 1, count), lambda m: (m, 0, 0)),
        ],
        out_specs=[
            pl.BlockSpec((count, att_width), lambda m: (m, 0)),
            pl.BlockSpec((HEADS, count, count), lambda m: (m, 0, 0)),
        ],
        out_shape=[
            jax.ShapeDtypeStruct((micro * count, att_width), BF16),
            jax.ShapeDtypeStruct((micro * HEADS, count, count), F32),
        ],
        cost_estimate=pl.CostEstimate(
            flops=4 * micro * HEADS * count * count * HEAD_DIM,
            bytes_accessed=micro * HEADS * count * count * 6,
            transcendentals=micro * HEADS * count * count,
        ),
        name="attend",
    )(projected, ids.reshape(micro * count, 1), ids.reshape(micro, 1, count))


def attend_back_kernel(proj_ref, prob_ref, datt_ref, dproj_ref, inner_ref):
    width = HEADS * HEAD_DIM
    keys = proj_ref[:, width : width + HEAD_DIM]
    values = proj_ref[:, width + HEAD_DIM :]
    grad_keys = None
    grad_values = None
    dot_total = 0.0
    for head in range(HEADS):
        part = slice(head * HEAD_DIM, (head + 1) * HEAD_DIM)
        probs = prob_ref[head]
        queries = proj_ref[:, part]
        d_att = datt_ref[:, part]
        d_probs = contract(d_att, values, 1, 1)
        row_inner = jnp.sum(d_probs * probs, axis=1, keepdims=True)
        d_scores = (probs * (d_probs - row_inner) * HEAD_DIM ** (-0.5)).astype(BF16)
        grad_q = contract(d_scores, keys, 1, 0).astype(BF16)
        dproj_ref[:, part] = grad_q
        dot_total = dot_total + grad_q.astype(F32) * queries.astype(F32)
        add_k = contract(d_scores, queries, 0, 0)
        add_v = contract(probs.astype(BF16), d_att, 0, 0)
        grad_keys = add_k if grad_keys is None else grad_keys + add_k
        grad_values = add_v if grad_values is None else grad_values + add_v
    grad_keys = grad_keys.astype(BF16)
    grad_values = grad_values.astype(BF16)
    dproj_ref[:, width : width + HEAD_DIM] = grad_keys
    dproj_ref[:, width + HEAD_DIM :] = grad_values
    dot_total = dot_total + grad_keys.astype(F32) * keys.astype(F32)
    dot_total = dot_total + grad_values.astype(F32) * values.astype(F32)
    inner_ref[...] = jnp.sum(dot_total, axis=1, keepdims=True)


def attend_back(projected, probs, d_att):
    total, width = projected.shape
    count = probs.shape[1]
    micro = total // count
    att_width = HEADS * HEAD_DIM
    return pl.pallas_call(
        attend_back_kernel,
        grid=(micro,),
        in_specs=[
            pl.BlockSpec((count, width), lambda m: (m, 0)),
            pl.BlockSpec((HEADS, count, count), lambda m: (m, 0, 0)),
            pl.BlockSpec((count, att_width), lambda m: (m, 0)),
        ],
        out_specs=[
            pl.BlockSpec((count, width), lambda m: (m, 0)),
            pl.BlockSpec((count, 1), lambda m: (m, 0)),
        ],
        out_shape=[
            jax.ShapeDtypeStruct((total, width), BF16),
            jax.ShapeDtypeStruct((total, 1), F32),
        ],
        cost_estimate=pl.CostEstimate(
            flops=8 * micro * HEADS * count * count * HEAD_DIM,
            bytes_accessed=micro * HEADS * count * count * 6,
            transcendentals=0,
        ),
        name="attend_back",
    )(projected, probs, d_att)


def normalize(tokens, gain_row):
    wide = tokens.astype(F32)
    inv_rms = lax.rsqrt(jnp.mean(wide * wide, axis=1, keepdims=True) + 1e-05)
    return inv_rms, (wide * inv_rms * gain_row).astype(BF16)


def body(
    x_forward,
    seg_forward,
    x_saved,
    x_earlier,
    cotangent,
    seg_backward,
    gain,
    qkv,
    proj,
    sum_gain,
    sum_qkv,
    sum_proj,
):
    x_next = shifted(x_earlier, "blk", -1)
    ids_next_b = shifted(seg_backward, "blk", -1)
    ids_next_f = shifted(seg_forward, "blk", -1)
    qkv_all = lax.all_gather(qkv[0], "fsdp", axis=0, tiled=True)
    gain_all = lax.all_gather(gain, "fsdp", axis=1, tiled=True).astype(F32)
    proj_all = lax.all_gather(proj[0], "fsdp", axis=1, tiled=True)

    features = x_saved.shape[1]
    inv_one, normed_one = normalize(x_saved, gain_all)
    inv_two, normed_two = normalize(x_next, gain_all)
    inv_fwd, normed_fwd = normalize(x_forward, gain_all)

    def project(normed):
        return jnp.dot(normed, qkv_all, preferred_element_type=F32).astype(BF16)

    proj_one = project(normed_one)
    att_one, probs_one = attend(proj_one, seg_backward)
    proj_fwd = project(normed_fwd)
    att_fwd, unused = attend(proj_fwd, seg_forward)
    proj_two = project(normed_two)
    att_two, probs_two = attend(proj_two, ids_next_b)

    d_att = contract(cotangent, proj_all, 1, 1).astype(BF16)
    d_proj_one, inner = attend_back(proj_one, probs_one, d_att)
    d_normed = contract(d_proj_one, qkv_all, 1, 1)
    d_hidden = (
        cotangent.astype(F32)
        + inv_one * gain_all * d_normed
        - x_saved.astype(F32) * (inv_one * inv_one * inner / features)
    ).astype(BF16)
    upstream = shifted(d_hidden, "blk", -1)

    hidden = (
        x_forward.astype(F32) + jnp.dot(att_fwd, proj_all, preferred_element_type=F32)
    ).astype(BF16)
    hidden_next = shifted(hidden, "blk", -1)

    d_att_two = contract(upstream, proj_all, 1, 1).astype(BF16)
    grad_proj = contract(
        jnp.concatenate([att_one, att_two], axis=0),
        jnp.concatenate([cotangent, upstream], axis=0),
        0,
        0,
    ).astype(BF16)
    reduced_proj = lax.psum_scatter(grad_proj, "fsdp", scatter_dimension=1, tiled=True)
    d_proj_two, unused = attend_back(proj_two, probs_two, d_att_two)
    grad_qkv = contract(
        jnp.concatenate([normed_one, normed_two], axis=0),
        jnp.concatenate([d_proj_one, d_proj_two], axis=0),
        0,
        0,
    ).astype(BF16)
    reduced_qkv = lax.psum_scatter(grad_qkv, "fsdp", scatter_dimension=0, tiled=True)

    inv_last, normed_last = normalize(hidden_next, gain_all)
    proj_last = project(normed_last)
    att_last, unused = attend(proj_last, ids_next_f)
    result = (
        hidden_next.astype(F32) + jnp.dot(att_last, proj_all, preferred_element_type=F32)
    ).astype(BF16)
    result = shifted(result, "blk", 1)

    new_proj = shifted((sum_proj[0] + reduced_proj.astype(F32)).astype(BF16), "blk", 1)
    wide_qkv = reduced_qkv.astype(F32)
    grad_gain = jnp.sum(wide_qkv * qkv[0].astype(F32), axis=1)[None] / gain.astype(F32)
    new_gain = shifted(sum_gain + grad_gain, "blk", 1)
    new_qkv = shifted((sum_qkv[0] + wide_qkv).astype(BF16), "blk", 1)
    return (result, new_gain, new_qkv.astype(F32)[None], new_proj.astype(F32)[None])


def solution(mesh):
    rows = P(("blk", "fsdp"), None)
    weights = (P("blk", "fsdp"), P("blk", "fsdp", None), P("blk", None, "fsdp"))
    return jax.shard_map(
        body,
        mesh=mesh,
        in_specs=(rows,) * 6 + weights + weights,
        out_specs=(rows,) + weights,
        check_vma=False,
    )
```

time: 694 us -> 503 us (0.72); the launches traced: 684 us -> 503 us
  waiting for transfers between devices: 522 us -> 350 us
  matrix products: 93 us -> 62.8 us
  Pallas kernels: 0 us -> 20.2 us
  starting transfers between devices: 3.37 us -> 10.8 us
    reduce_scatter x4 -> x2, waiting for transfers between devices: 216 us -> 120 us  [the longest x1 75 us: body(): lax.psum_scatter(grad_proj, 'fsdp', scatter_dimension=1, tiled=True)]
    ppermute x6 -> x9, waiting for transfers between devices: 107 us -> 67.8 us  [shifted(): return lax.ppermute(value, axis, pairs)]
    dot_general x26 -> x11, matrix products: 86.7 us -> 62.8 us  [the longest x5 30.4 us: contract(): lax.dot_general(a, b, (((dim_a,), (dim_b,)), ((), ())), preferred_element...]
    pallas_call x0 -> x6, Pallas kernels: none -> 20.2 us  [the longest x4 12.6 us: attend(): pl.pallas_call(attend_kernel, grid=(micro,), in_specs=[pl.BlockSpec((coun...]
    all_gather x2, waiting for transfers between devices: 179 us -> 160 us  [the longest x1 111 us: body(): qkv_all = lax.all_gather(qkv[0], 'fsdp', axis=0, tiled=True)]
    unnamed x10 -> x4, waiting for transfers between devices: 19.8 us -> 1.41 us
    ppermute x6 -> x9, starting transfers between devices: 2.88 us -> 10.4 us  [shifted(): return lax.ppermute(value, axis, pairs)]
    add x3 -> x1, other arithmetic: 7.42 us -> 0.01 us  [body(): new_gain = shifted(sum_gain + grad_gain, 'blk', 1)]
  transfers between devices with their start and end apart: 14 -> 13, of which waited for: 7 -> 8; matrix products, arithmetic and copies ran while one was open for 13% -> 12% of each run, Pallas kernels for 0% -> 2%
where the time goes in v1:
time: 503 us
  waiting for transfers between devices  350 us (70%)
  matrix products  62.8 us (12%)
  other arithmetic  22.4 us (4%)
  Pallas kernels  20.2 us (4%)
  between operations  13.9 us (3%)
  blocking collectives  13.7 us (3%)
  starting transfers between devices  10.8 us (2%)
  local copies, waits for them, and re-layouts  9.27 us (2%)
    all_gather x1, waiting for transfers between devices, body(): qkv_all = lax.all_gather(qkv[0], 'fsdp', axis=0, tiled=True)  111 us
    reduce_scatter x1, waiting for transfers between devices, body(): lax.psum_scatter(grad_proj, 'fsdp', scatter_dimension=1, tiled=True)  75 us
    ppermute x9, waiting for transfers between devices, shifted(): return lax.ppermute(value, axis, pairs)  67.8 us
    all_gather x1, waiting for transfers between devices, body(): proj_all = lax.all_gather(proj[0], 'fsdp', axis=1, tiled=True)  49.8 us
    reduce_scatter x1, waiting for transfers between devices, body(): lax.psum_scatter(grad_qkv, 'fsdp', scatter_dimension=0, tiled=True)  45.1 us
    dot_general x5, matrix products, contract(): lax.dot_general(a, b, (((dim_a,), (dim_b,)), ((), ())), preferred_element...  30.4 us
    dot_general x4, matrix products, project(): return jnp.dot(normed, qkv_all, preferred_element_type=F32).astype(BF16)  22.7 us
    all_gather x1, blocking collectives, body(): gain_all = lax.all_gather(gain, 'fsdp', axis=1, tiled=True).astype(F32)  13.7 us
  transfers between devices with their start and end apart: 13, of which 8 were waited for; matrix products, arithmetic and copies ran while one was open for 12% of the time, Pallas kernels for 2%

profile of v1, /device:TPU:0, one launch (start us, length us, event | category | flops | bytes accessed | tf_op | source)
XLA Modules:
  0.0 502.6 jit_solution(6170129560086756209)
XLA Ops:
  7.2 0.0 copy-start.5
  7.2 0.0 all-gather.7.cloned.1.call-start
  7.2 0.7 all-gather.7.cloned.1.call-update
  7.9 0.0 all-gather.5.cloned.1.call-start
  8.0 0.7 all-gather.5.cloned.1.call-update
  8.7 0.0 reduce-scatter.3.cloned.1.call-start
  8.7 3.4 collective-permute-start.3
  12.1 13.7 %all_gather.9 = bf16[1,4096]{1,0:T(2,128)(2,1)S(1)} all-gather(bf16[1,1024]{1,0:T(2,128)(2,1)} %param.18), channel_id=1, replica_groups=mesh['blk'=8,'fsdp'=4] {'fsdp'}, dimensions={1}, use_global_device_ids=true | all-gather | bytes 10240 | tf_op jit(solution)/shard_map/all_gather | solution.py:157
  25.8 2.1 fusion.33
  27.9 0.1 copy.20
  28.1 0.8 copy.18.col_ref
  28.9 7.1 %collective-permute-done.3 = bf16[256,4096]{1,0:T(8,128)(2,1)} collective-permute-done((bf16[256,4096]{1,0:T(8,128)(2,1)}, bf16[256,4096]{1,0:T(8,128)(2,1)}, u32[]{:S(2)}, u32[]{:S(2)}) %collective-permute-start.3) | collective-permute-done | bytes 2097184 | tf_op jit(solution)/shard_map/ppermute | solution.py:17
  36.0 2.1 fusion.24
  38.1 5.2 %fusion.35 = (bf16[256,4096]{1,0:T(8,128)(2,1)}, bf16[256,4096]{1,0:T(8,128)(2,1)}) fusion(bf16[256,4096]{1,0:T(8,128)(2,1)S(1)} %copy-done, f32[256]{0:T(256)S(1)} %get-tuple-element.27, f32[4096]{0:T(1024)S(1)} %bitcast.73, f32[256]{0:T(256)S(1)} %add_rsqrt_fusion, bf16[256,4096]{1,0:T(8,128)(2,1)} %collective-permute-done.3), kind=kLoop, calls=%fused_computation.40 | loop fusion | flops 8388608 | bytes 8407040 | tf_op jit(solution)/shard_map/convert_element_type | solution.py:136
  43.3 49.8 %all-gather.7.cloned.1.call-done = bf16[1,512,4096]{2,1,0:T(8,128)(2,1)} async-done(((bf16[1,512,1024]{2,1,0:T(8,128)(2,1)}), bf16[1,512,4096]{2,1,0:T(8,128)(2,1)}) %all-gather.7.cloned.1.call-update) | async-done | bytes 4194320 | tf_op jit(solution)/shard_map/all_gather | solution.py:158
  93.1 4.8 fusion.73.datt_ref
  97.9 110.5 %all-gather.5.cloned.1.call-done = bf16[1,4096,768]{2,1,0:T(8,128)(2,1)} async-done(((bf16[1,1024,768]{2,1,0:T(8,128)(2,1)}), bf16[1,4096,768]{2,1,0:T(8,128)(2,1)}) %all-gather.5.cloned.1.call-update) | async-done | bytes 6291472 | tf_op jit(solution)/shard_map/all_gather | solution.py:156
  208.5 6.0 %fusion.67.proj_ref = bf16[256,768]{1,0:T(8,128)(2,1)} fusion(bf16[256,4096]{1,0:T(8,128)(2,1)} %get-tuple-element.24, bf16[1,4096,768]{2,1,0:T(8,128)(2,1)} %all-gather.5.cloned.1.call-done), kind=kOutput, calls=%fused_computation.66 | convolution fusion | flops 1610809344 | bytes 8781824 | tf_op jit(solution)/shard_map/dot_general | solution.py:166
  214.4 3.1 attend.6
  217.6 3.9 attend_back.2
  221.4 1.0 multiply_reduce_fusion
  222.4 0.0 copy-start.6
  222.5 7.0 %fusion.21 = bf16[256,4096]{1,0:T(8,128)(2,1)} fusion(bf16[256,768]{1,0:T(8,128)(2,1)} %get-tuple-element.16, bf16[1,4096,768]{2,1,0:T(8,128)(2,1)} %all-gather.5.cloned.1.call-done, bf16[256,4096]{1,0:T(8,128)(2,1)S(1)} %copy-done, bf16[256,4096]{1,0:T(8,128)(2,1)} %param.16, f32[256]{0:T(256)S(1)} %multiply_reduce_fusion, f32[256]{0:T(256)S(1)} %get-tuple-element.27, ...), kind=kOutput, calls=%fused_computation.28 | convolution fusion | flops 1619001344 | bytes 12994560 | tf_op jit(solution)/shard_map/dot_general | solution.py:21
  229.4 2.0 collective-permute-start.5
  231.4 0.5 collective-permute-start.4
  231.9 23.4 %collective-permute-done.4 = s32[1,256]{1,0:T(1,128)S(1)} collective-permute-done((s32[1,256]{1,0:T(1,128)S(1)}, s32[1,256]{1,0:T(1,128)S(1)}, u32[]{:S(2)}, u32[]{:S(2)}) %collective-permute-start.4) | collective-permute-done | bytes 1056 | tf_op jit(solution)/shard_map/ppermute | solution.py:17
  255.3 0.8 copy.19.col_ref
  256.1 6.0 %fusion.70.proj_ref = bf16[256,768]{1,0:T(8,128)(2,1)} fusion(bf16[256,4096]{1,0:T(8,128)(2,1)} %get-tuple-element.25, bf16[1,4096,768]{2,1,0:T(8,128)(2,1)} %all-gather.5.cloned.1.call-done), kind=kOutput, calls=%fused_computation.67 | convolution fusion | flops 1610809344 | bytes 8781824 | tf_op jit(solution)/shard_map/dot_general | solution.py:166
  262.0 3.2 attend.7
  265.2 5.0 fusion.76.datt_ref
  270.2 3.8 attend_back.3
  274.0 7.7 %convolution_convert_fusion = bf16[4096,768]{1,0:T(8,128)(2,1)} fusion(bf16[256,4096]{1,0:T(8,128)(2,1)} %get-tuple-element.25, bf16[256,4096]{1,0:T(8,128)(2,1)S(1)} %copy-done.2, bf16[256,768]{1,0:T(8,128)(2,1)} %get-tuple-element.19, bf16[256,768]{1,0:T(8,128)(2,1)S(1)} %copy-done.13), kind=kOutput, calls=%fused_computation | convolution fusion | flops 3234332672 | bytes 11272192 | tf_op jit(solution)/shard_map/dot_general | solution.py:21
  281.7 0.0 reduce-scatter.3.cloned.1.call-update
  281.8 0.3 reduce-scatter.5.cloned.1.call-start
  282.0 1.3 copy-done.12
  283.3 0.1 copy-done.15
  283.4 5.9 %convolution_convert_fusion.1 = bf16[512,4096]{1,0:T(8,128)(2,1)} fusion(bf16[256,4096]{1,0:T(8,128)(2,1)} %collective-permute-done.5, bf16[256,4096]{1,0:T(8,128)(2,1)S(1)} %copy-done.12, bf16[256,512]{1,0:T(8,128)(2,1)S(1)} %copy-done.15, bf16[256,512]{1,0:T(8,128)(2,1)S(1)} %copy-done.14), kind=kOutput, calls=%fused_computation.20 | convolution fusion | flops 2159017984 | bytes 8912896 | tf_op jit(solution)/shard_map/dot_general | solution.py:21
  289.3 0.0 reduce-scatter.5.cloned.1.call-update
  289.3 0.7 copy-done.7
  290.0 0.8 copy.16.col_ref
  290.8 0.1 copy-done.1
  290.9 0.5 fusion.27
  291.4 5.4 %fusion.57.proj_ref = bf16[256,768]{1,0:T(8,128)(2,1)} fusion(bf16[1,4096,768]{2,1,0:T(8,128)(2,1)} %all-gather.5.cloned.1.call-done, bf16[256,4096]{1,0:T(8,128)(2,1)S(1)} %copy-done.1, f32[4096]{0:T(1024)S(1)} %bitcast.75, f32[256]{0:T(256)S(1)} %add_rsqrt_fusion.3), kind=kOutput, calls=%fused_computation.64 | convolution fusion | flops 1615003648 | bytes 8799232 | tf_op jit(solution)/shard_map/dot_general | solution.py:166
  296.8 3.1 attend.4
  299.9 4.9 fusion.19
  304.8 2.8 collective-permute-start
  307.6 0.0 collective-permute-start.1
  307.6 23.8 %collective-permute-done.1 = s32[1,256]{1,0:T(1,128)S(1)} collective-permute-done((s32[1,256]{1,0:T(1,128)S(1)}, s32[1,256]{1,0:T(1,128)S(1)}, u32[]{:S(2)}, u32[]{:S(2)}) %collective-permute-start.1) | collective-permute-done | bytes 1056 | tf_op jit(solution)/shard_map/ppermute | solution.py:17
  331.5 0.8 copy.17.col_ref
  332.3 0.5 fusion.30
  332.8 5.4 %fusion.62.proj_ref = bf16[256,768]{1,0:T(8,128)(2,1)} fusion(bf16[1,4096,768]{2,1,0:T(8,128)(2,1)} %all-gather.5.cloned.1.call-done, bf16[256,4096]{1,0:T(8,128)(2,1)S(1)} %collective-permute-done, f32[256]{0:T(256)S(1)} %add_rsqrt_fusion.2, f32[4096]{0:T(1024)S(1)} %bitcast.76), kind=kOutput, calls=%fused_computation.65 | convolution fusion | flops 1615003648 | bytes 8799232 | tf_op jit(solution)/shard_map/dot_general | solution.py:166
  338.2 3.1 attend.5
  341.3 4.9 fusion.20
  346.2 45.1 %reduce-scatter.3.cloned.1.call-done = bf16[1024,768]{1,0:T(8,128)(2,1)} async-done(((bf16[4096,768]{1,0:T(8,128)(2,1)}), bf16[1024,768]{1,0:T(8,128)(2,1)}) %reduce-scatter.3.cloned.1.call-update) | async-done | bytes 1572880 | tf_op jit(solution)/shard_map/reduce_scatter | solution.py:205
  391.3 4.5 fusion.49
  395.8 75.0 %reduce-scatter.5.cloned.1.call-done = bf16[512,1024]{1,0:T(8,128)(2,1)} async-done(((bf16[512,4096]{1,0:T(8,128)(2,1)}), bf16[512,1024]{1,0:T(8,128)(2,1)}) %reduce-scatter.5.cloned.1.call-update) | async-done | bytes 1048592 | tf_op jit(solution)/shard_map/reduce_scatter | solution.py:197
  470.8 1.6 fusion.52
  472.3 0.1 collective-permute-start.8
  472.5 1.6 collective-permute-start.6
  474.1 13.4 %collective-permute-done.8 = bf16[512,1024]{1,0:T(8,128)(2,1)S(1)} collective-permute-done((bf16[512,1024]{1,0:T(8,128)(2,1)S(1)}, bf16[512,1024]{1,0:T(8,128)(2,1)S(1)}, u32[]{:S(2)}, u32[]{:S(2)}) %collective-permute-start.8) | collective-permute-done | bytes 1048608 | tf_op jit(solution)/shard_map/ppermute | solution.py:17
  487.5 1.6 bitcast_convert_fusion.1
  489.1 3.3 bitcast_convert_fusion
  492.4 3.1 copy.23
  495.5 0.6 copy.24
  (39 shorter events, 0.1 us)
Async XLA Ops:
  7.2 30.9 %copy-start = (bf16[256,4096]{1,0:T(8,128)(2,1)S(1)}, bf16[256,4096]{1,0:T(8,128)(2,1)}, u32[]{:S(2)}) copy-start(bf16[256,4096]{1,0:T(8,128)(2,1)} %param.14) | copy-start | bytes 6291460
  7.2 20.9 %copy-start.5 = (s32[1,256]{1,0:T(1,128)S(1)}, s32[1,256]{1,0:T(1,128)}, u32[]{:S(2)}) copy-start(s32[1,256]{1,0:T(1,128)} %param.17) | copy-start | bytes 3076
  7.2 85.9 %all-gather.7.cloned.1.call-start = ((), (), s32[]{:S(2)}) async-start(), calls=%async_computation.5 | async-start | bytes 5242880 | tf_op jit(solution)/shard_map/all_gather | solution.py:158
  7.9 200.6 %all-gather.5.cloned.1.call-start = ((), (), s32[]{:S(2)}) async-start(), calls=%async_computation.4 | async-start | bytes 7864320 | tf_op jit(solution)/shard_map/all_gather | solution.py:156
  8.7 382.6 %reduce-scatter.3.cloned.1.call-start = ((), (), s32[]{:S(2)}) async-start(), calls=%async_computation.2 | async-start | bytes 7864320 | tf_op jit(solution)/shard_map/reduce_scatter | solution.py:205
  8.7 27.3 %collective-permute-start.3 = (bf16[256,4096]{1,0:T(8,128)(2,1)}, bf16[256,4096]{1,0:T(8,128)(2,1)}, u32[]{:S(2)}, u32[]{:S(2)}) collective-permute-start(bf16[256,4096]{1,0:T(8,128)(2,1)} %param.15), channel_id=1, source_target_pairs={{0,28},{4,0},{8,4},{12,8},{16,12},{20,16},{24,20},{28,24},{1,29},{... | collective-permute-start | bytes 6291464 | tf_op jit(solution)/shard_map/ppermute | solution.py:17
  222.4 9.0 %copy-start.6 = (s32[1,256]{1,0:T(1,128)S(1)}, s32[1,256]{1,0:T(1,128)}, u32[]{:S(2)}) copy-start(s32[1,256]{1,0:T(1,128)} %param.17) | copy-start | bytes 3076
  229.4 35.8 %collective-permute-start.5 = (bf16[256,4096]{1,0:T(8,128)(2,1)}, bf16[256,4096]{1,0:T(8,128)(2,1)}, u32[]{:S(2)}, u32[]{:S(2)}) collective-permute-start(bf16[256,4096]{1,0:T(8,128)(2,1)} %fusion.21), channel_id=1, source_target_pairs={{0,28},{4,0},{8,4},{12,8},{16,12},{20,16},{24,20},{28,24},{1,29},{... | collective-permute-start | bytes 6291464 | tf_op jit(solution)/shard_map/ppermute | solution.py:17
  231.4 23.9 %collective-permute-start.4 = (s32[1,256]{1,0:T(1,128)S(1)}, s32[1,256]{1,0:T(1,128)S(1)}, u32[]{:S(2)}, u32[]{:S(2)}) collective-permute-start(s32[1,256]{1,0:T(1,128)S(1)} %copy-done.6), channel_id=1, source_target_pairs={{0,28},{4,0},{8,4},{12,8},{16,12},{20,16},{24,20},{28,24},{1,29},{... | collective-permute-start | bytes 3080 | tf_op jit(solution)/shard_map/ppermute | solution.py:17
  255.3 6.8 %copy-start.10 = (s32[1,256]{1,0:T(1,128)}, s32[1,256]{1,0:T(1,128)S(1)}, u32[]{:S(2)}) copy-start(s32[1,256]{1,0:T(1,128)S(1)} %collective-permute-done.4) | copy-start | bytes 3076
  265.2 8.8 %copy-start.2 = (bf16[256,4096]{1,0:T(8,128)(2,1)S(1)}, bf16[256,4096]{1,0:T(8,128)(2,1)}, u32[]{:S(2)}) copy-start(bf16[256,4096]{1,0:T(8,128)(2,1)} %get-tuple-element.24) | copy-start | bytes 6291460
  265.2 8.8 %copy-start.13 = (bf16[256,768]{1,0:T(8,128)(2,1)S(1)}, bf16[256,768]{1,0:T(8,128)(2,1)}, u32[]{:S(2)}) copy-start(bf16[256,768]{1,0:T(8,128)(2,1)} %get-tuple-element.16) | copy-start | bytes 1179652
  281.7 1.6 copy-start.12
  281.7 1.6 copy-start.14
  281.7 1.7 copy-start.15
  281.8 189.0 %reduce-scatter.5.cloned.1.call-start = ((), (), s32[]{:S(2)}) async-start(), calls=%async_computation.3 | async-start | bytes 5242880 | tf_op jit(solution)/shard_map/reduce_scatter | solution.py:197
  289.3 0.7 copy-start.7
  289.3 1.6 copy-start.1
  299.9 7.7 %copy-start.8 = (s32[1,256]{1,0:T(1,128)S(1)}, s32[1,256]{1,0:T(1,128)}, u32[]{:S(2)}) copy-start(s32[1,256]{1,0:T(1,128)} %param.13) | copy-start | bytes 3076
  304.8 27.5 %collective-permute-start = (bf16[256,4096]{1,0:T(8,128)(2,1)}, bf16[256,4096]{1,0:T(8,128)(2,1)S(1)}, u32[]{:S(2)}, u32[]{:S(2)}) collective-permute-start(bf16[256,4096]{1,0:T(8,128)(2,1)} %fusion.19), channel_id=1, source_target_pairs={{0,28},{4,0},{8,4},{12,8},{16,12},{20,16},{24,20},{28,24},{1,29},{... | collective-permute-start | bytes 6291464 | tf_op jit(solution)/shard_map/ppermute | solution.py:17
  307.6 23.9 %collective-permute-start.1 = (s32[1,256]{1,0:T(1,128)S(1)}, s32[1,256]{1,0:T(1,128)S(1)}, u32[]{:S(2)}, u32[]{:S(2)}) collective-permute-start(s32[1,256]{1,0:T(1,128)S(1)} %copy-done.8), channel_id=1, source_target_pairs={{0,28},{4,0},{8,4},{12,8},{16,12},{20,16},{24,20},{28,24},{1,29},{... | collective-permute-start | bytes 3080 | tf_op jit(solution)/shard_map/ppermute | solution.py:17
  331.5 6.7 %copy-start.9 = (s32[1,256]{1,0:T(1,128)}, s32[1,256]{1,0:T(1,128)S(1)}, u32[]{:S(2)}) copy-start(s32[1,256]{1,0:T(1,128)S(1)} %collective-permute-done.1) | copy-start | bytes 3076
  346.2 124.6 %copy-start.3 = (f32[1,512,1024]{2,1,0:T(8,128)S(1)}, f32[1,512,1024]{2,1,0:T(8,128)}, u32[]{:S(2)}) copy-start(f32[1,512,1024]{2,1,0:T(8,128)} %param.23) | copy-start | bytes 6291460
  346.2 126.3 %copy-start.4 = (bf16[1,1024]{1,0:T(2,128)(2,1)S(1)}, bf16[1,1024]{1,0:T(2,128)(2,1)}, u32[]{:S(2)}) copy-start(bf16[1,1024]{1,0:T(2,128)(2,1)} %param.18) | copy-start | bytes 6148
  346.2 126.3 %copy-start.11 = (f32[1,1024]{1,0:T(1,128)S(1)}, f32[1,1024]{1,0:T(1,128)}, u32[]{:S(2)}) copy-start(f32[1,1024]{1,0:T(1,128)} %param.21) | copy-start | bytes 12292
  346.2 126.2 %collective-permute-start.2 = (bf16[256,4096]{1,0:T(8,128)(2,1)}, bf16[256,4096]{1,0:T(8,128)(2,1)}, u32[]{:S(2)}, u32[]{:S(2)}) collective-permute-start(bf16[256,4096]{1,0:T(8,128)(2,1)} %fusion.20), channel_id=1, source_target_pairs={{0,4},{4,8},{8,12},{12,16},{16,20},{20,24},{24,28},{28,0},{1,5},{5... | collective-permute-start | bytes 6291464 | tf_op jit(solution)/shard_map/ppermute | solution.py:17
  395.8 93.3 %collective-permute-start.7 = (bf16[1024,768]{1,0:T(8,128)(2,1)}, bf16[1024,768]{1,0:T(8,128)(2,1)}, u32[]{:S(2)}, u32[]{:S(2)}) collective-permute-start(bf16[1024,768]{1,0:T(8,128)(2,1)} %get-tuple-element.22), channel_id=1, source_target_pairs={{0,4},{4,8},{8,12},{12,16},{16,20},{20,24},{24,28},{28,0},{1,5},{5... | collective-permute-start | bytes 4718600 | tf_op jit(solution)/shard_map/ppermute | solution.py:17
  472.3 15.2 %collective-permute-start.8 = (bf16[512,1024]{1,0:T(8,128)(2,1)S(1)}, bf16[512,1024]{1,0:T(8,128)(2,1)S(1)}, u32[]{:S(2)}, u32[]{:S(2)}) collective-permute-start(bf16[512,1024]{1,0:T(8,128)(2,1)S(1)} %fusion.52), channel_id=1, source_target_pairs={{0,4},{4,8},{8,12},{12,16},{16,20},{20,24},{24,28},{28,0},{1,5},{5... | collective-permute-start | bytes 3145736 | tf_op jit(solution)/shard_map/ppermute | solution.py:17
  472.5 16.6 %collective-permute-start.6 = (f32[1,1024]{1,0:T(1,128)S(1)}, f32[1,1024]{1,0:T(1,128)S(1)}, u32[]{:S(2)}, u32[]{:S(2)}) collective-permute-start(f32[1,1024]{1,0:T(1,128)S(1)} %divide_add_fusion), channel_id=1, source_target_pairs={{0,4},{4,8},{8,12},{12,16},{16,20},{20,24},{24,28},{28,0},{1,5},{5... | collective-permute-start | bytes 12296 | tf_op jit(solution)/shard_map/ppermute | solution.py:17
Sparse Core Ops, SparseCore 0:
  9.6 83.4 all-gather.6
  94.7 113.7 all-gather.4
  281.9 109.3 reduce-scatter.2
  393.4 77.2 reduce-scatter.4
